TPU v7x, 512 devices: a whole 4x8x8 slice. The times are simulated.
512 devices in a mesh: row: 16 (over z, core), col: 32 (over y, x).
Axes of the slice: x: 4, y: 8, z: 8, core: 2. Of those that a mesh axis runs over, the one named last changes fastest.
Arguments:
- embeddings: bfloat16 [2048, 512], P('row'), may hold values from -6 to 6
- row_weight: bfloat16 [512, 32], replicated, may hold values from -0.25 to 0.25
- col_weight: bfloat16 [512, 32], replicated, may hold values from -0.25 to 0.25
- conv_weights: bfloat16 [3, 32, 32, 3, 3], replicated, may hold values from -0.5 to 0.5
- conv_bias: float32 [3, 32], replicated, may hold values from -3 to 3
- head_weight: bfloat16 [32], replicated, may hold values from -1 to 1
Outputs:
- contact_map: float32 [2048, 2048], P('row', 'col')
All inputs are finite; a program needn't handle non-finite values.
Results may differ from a plain program's by a relative error of at most 0.023.
Values may be sent and summed in bfloat16 or wider, within the bound.
A program may use at most 64 MiB of HBM per device.

v0:
```python
import jax
import jax.numpy as jnp
from jax import lax
from jax.sharding import PartitionSpec as P


def spread(value, axis, source):
    kept = jnp.where(lax.axis_index(axis) == source, value, 0).astype(value.dtype)
    return lax.psum(kept, axis)


def extended(cells, sides, width):
    for axis, dim in sides:
        count = lax.axis_size(axis)
        ends = count - 1
        head = lax.slice_in_dim(cells, 0, width, axis=dim)
        tail = lax.slice_in_dim(cells, cells.shape[dim] - width, cells.shape[dim], axis=dim)
        cells = jnp.concatenate(
            [
                lax.ppermute(tail, axis, [(i, (i + 1) % count) for i in range(ends)]),
                cells,
                lax.ppermute(head, axis, [((i + 1) % count, i) for i in range(ends)]),
            ],
            axis=dim,
        )
    return cells


def dilated_level(padded, weight, level_bias, dilation):
    summed = lax.conv_general_dilated(
        padded[None],
        weight,
        (1, 1),
        "VALID",
        rhs_dilation=(dilation, dilation),
        dimension_numbers=("NCHW", "OIHW", "NCHW"),
        preferred_element_type=jnp.float32,
    )[0]
    return jax.nn.relu(summed + level_bias[:, None, None]).astype(jnp.bfloat16)


def pair_tile(rows_part, cols_part):
    return (
        rows_part.T.astype(jnp.float32)[:, :, None] + cols_part.T.astype(jnp.float32)[:, None, :]
    ).astype(jnp.bfloat16)


def body(embeddings, row_weight, col_weight, conv_weights, conv_bias, head_weight):
    row_bins = embeddings.shape[0]
    total_bins = row_bins * lax.axis_size("row")
    col_bins = total_bins // lax.axis_size("col")
    first_col = lax.axis_index("col") * col_bins
    owner_row = first_col // row_bins
    offset = first_col - owner_row * row_bins
    dilations = (1, 2, 4)
    row_feats = jnp.dot(embeddings, row_weight, preferred_element_type=jnp.float32).astype(
        jnp.bfloat16
    )
    owner_block = spread(embeddings, "row", owner_row)
    col_rows = lax.dynamic_slice_in_dim(owner_block, offset, col_bins, 0)
    col_feats = jnp.dot(col_rows, col_weight, preferred_element_type=jnp.float32).astype(
        jnp.bfloat16
    )
    current = pair_tile(row_feats, col_feats)
    for level_number, dilation in enumerate(dilations):
        padded = extended(current, (("row", 1), ("col", 2)), dilation)
        current = dilated_level(
            padded, conv_weights[level_number], conv_bias[level_number], dilation
        )
    return jnp.einsum("c,crj->rj", head_weight, current, preferred_element_type=jnp.float32)


def solution(mesh):
    return jax.shard_map(
        body,
        mesh=mesh,
        in_specs=(P("row", None), P(), P(), P(), P(), P()),
        out_specs=P("row", "col"),
        check_vma=False,
    )
```

profile of v0, /device:TPU:223, one launch (start us, length us, event | category | flops | bytes accessed | tf_op | source)
XLA Modules:
  0.0 261.4 jit_solution(6402877888625267361)
XLA Ops:
  9.2 117.9 %all-reduce.2.cloned.1.call-done = bf16[128,512]{1,0:T(8,128)(2,1)} async-done(((bf16[128,512]{1,0:T(8,128)(2,1)}), bf16[128,512]{1,0:T(8,128)(2,1)}) %all-reduce.2.cloned.1.call-update) | async-done | bytes 131088 | tf_op jit(solution)/shard_map/psum | solution.py:9
  128.7 4.1 %collective-permute-start = (bf16[32,1,64]{1,0,2:T(8,128)(2,1)S(1)}, bf16[32,1,64]{1,0,2:T(8,128)(2,1)S(1)}, u32[]{:S(2)}, u32[]{:S(2)}) collective-permute-start(bf16[32,1,64]{1,0,2:T(8,128)(2,1)S(1)} %get-tuple-element.15), channel_id=1, source_target_pairs={{0,32},{32,64},{64,96},{96,128},{128,160},{160,192},{192,224},{224... | collective-permute-start | bytes 12296 | tf_op jit(solution)/shard_map/ppermute | solution.py:20
  132.8 1.9 collective-permute-start.1
  134.8 4.2 %collective-permute-done = bf16[32,1,64]{1,0,2:T(8,128)(2,1)S(1)} collective-permute-done((bf16[32,1,64]{1,0,2:T(8,128)(2,1)S(1)}, bf16[32,1,64]{1,0,2:T(8,128)(2,1)S(1)}, u32[]{:S(2)}, u32[]{:S(2)}) %collective-permute-start) | collective-permute-done | bytes 4128 | tf_op jit(solution)/shard_map/ppermute | solution.py:20
  138.9 5.6 %collective-permute-done.1 = bf16[32,1,64]{1,0,2:T(8,128)(2,1)S(1)} collective-permute-done((bf16[32,1,64]{1,0,2:T(8,128)(2,1)S(1)}, bf16[32,1,64]{1,0,2:T(8,128)(2,1)S(1)}, u32[]{:S(2)}, u32[]{:S(2)}) %collective-permute-start.1) | collective-permute-done | bytes 4128 | tf_op jit(solution)/shard_map/ppermute | solution.py:22
  144.6 4.3 %collective-permute-start.2 = (bf16[32,130,1]{1,0,2:T(8,128)(2,1)S(1)}, bf16[32,130,1]{1,0,2:T(8,128)(2,1)S(1)}, u32[]{:S(2)}, u32[]{:S(2)}) collective-permute-start(bf16[32,130,1]{1,0,2:T(8,128)(2,1)S(1)} %get-tuple-element.9), channel_id=1, source_target_pairs={{0,1},{1,2},{2,3},{3,4},{4,5},{5,6},{6,7},{7,8},{8,9},{9,10},{10,1... | collective-permute-start | bytes 24968 | tf_op jit(solution)/shard_map/ppermute | solution.py:20
  149.0 1.9 collective-permute-start.3
  150.9 5.8 %collective-permute-done.3 = bf16[32,130,1]{1,0,2:T(8,128)(2,1)S(1)} collective-permute-done((bf16[32,130,1]{1,0,2:T(8,128)(2,1)S(1)}, bf16[32,130,1]{1,0,2:T(8,128)(2,1)S(1)}, u32[]{:S(2)}, u32[]{:S(2)}) %collective-permute-start.3) | collective-permute-done | bytes 8352 | tf_op jit(solution)/shard_map/ppermute | solution.py:22
  157.8 3.1 %copy.32 = bf16[32,130,1,8,9]{0,3,4,1,2:T(8,128)(2,1)} copy(bf16[32,130,1,8,9]{1,0,4,3,2:T(8,128)(2,1)S(1)} %bitcast.84) | data formatting | bytes 1198080 | tf_op jit(solution)/shard_map/conv_general_dilated | solution.py:30
  162.1 6.6 %broadcast_select_fusion.2 = f32[128,8,9,32]{3,1,2,0:T(8,128)} fusion(pred[8,9]{0,1:T(8,128)(4,1)S(1)} %copy-done.4, bf16[32,130,1,7,2]{0,3,4,1,2:T(8,128)(2,1)S(1)} %slice.80, bf16[32,130,1,8,9]{0,3,4,1,2:T(8,128)(2,1)} %copy.32, bf16[3,32,32,3,3]{2,1,4,3,0:T(8,128)(2,1)S(1)} %copy-done.3), kind=kOutput, calls=%fused_computation.27 | convolution fusion | flops 172360704 | bytes 2386944 | tf_op jit(solution)/shard_map/conv_general_dilated | solution.py:30
  168.6 3.7 %copy.33 = f32[128,8,9,32]{0,3,2,1:T(8,128)S(1)} copy(f32[128,8,9,32]{3,1,2,0:T(8,128)} %broadcast_select_fusion.2) | data formatting | bytes 2359296 | tf_op jit(solution)/shard_map/conv_general_dilated | solution.py:30
  172.8 3.2 %collective-permute-start.4 = (bf16[32,2,64]{1,0,2:T(8,128)(2,1)S(1)}, bf16[32,2,64]{1,0,2:T(8,128)(2,1)S(1)}, u32[]{:S(2)}, u32[]{:S(2)}) collective-permute-start(bf16[32,2,64]{1,0,2:T(8,128)(2,1)S(1)} %get-tuple-element.13), channel_id=1, source_target_pairs={{0,32},{32,64},{64,96},{96,128},{128,160},{160,192},{192,224},{224... | collective-permute-start | bytes 24584 | tf_op jit(solution)/shard_map/ppermute | solution.py:20
  176.0 1.9 collective-permute-start.5
  177.9 4.2 %collective-permute-done.4 = bf16[32,2,64]{1,0,2:T(8,128)(2,1)S(1)} collective-permute-done((bf16[32,2,64]{1,0,2:T(8,128)(2,1)S(1)}, bf16[32,2,64]{1,0,2:T(8,128)(2,1)S(1)}, u32[]{:S(2)}, u32[]{:S(2)}) %collective-permute-start.4) | collective-permute-done | bytes 8224 | tf_op jit(solution)/shard_map/ppermute | solution.py:20
  182.1 5.6 %collective-permute-done.5 = bf16[32,2,64]{1,0,2:T(8,128)(2,1)S(1)} collective-permute-done((bf16[32,2,64]{1,0,2:T(8,128)(2,1)S(1)}, bf16[32,2,64]{1,0,2:T(8,128)(2,1)S(1)}, u32[]{:S(2)}, u32[]{:S(2)}) %collective-permute-start.5) | collective-permute-done | bytes 8224 | tf_op jit(solution)/shard_map/ppermute | solution.py:22
  187.8 1.9 collective-permute-start.6
  189.7 3.4 %collective-permute-start.7 = (bf16[32,132,2]{1,0,2:T(8,128)(2,1)S(1)}, bf16[32,132,2]{1,0,2:T(8,128)(2,1)S(1)}, u32[]{:S(2)}, u32[]{:S(2)}) collective-permute-start(bf16[32,132,2]{1,0,2:T(8,128)(2,1)S(1)} %get-tuple-element.8), channel_id=1, source_target_pairs={{1,0},{2,1},{3,2},{4,3},{5,4},{6,5},{7,6},{8,7},{9,8},{10,9},{11,1... | collective-permute-start | bytes 50696 | tf_op jit(solution)/shard_map/ppermute | solution.py:22
  193.1 4.6 %collective-permute-done.7 = bf16[32,132,2]{1,0,2:T(8,128)(2,1)S(1)} collective-permute-done((bf16[32,132,2]{1,0,2:T(8,128)(2,1)S(1)}, bf16[32,132,2]{1,0,2:T(8,128)(2,1)S(1)}, u32[]{:S(2)}, u32[]{:S(2)}) %collective-permute-start.7) | collective-permute-done | bytes 16928 | tf_op jit(solution)/shard_map/ppermute | solution.py:22
  199.6 3.3 %copy.35 = bf16[32,132,1,8,9]{0,3,4,1,2:T(8,128)(2,1)S(1)} copy(bf16[32,132,1,8,9]{1,0,4,3,2:T(8,128)(2,1)} %bitcast.82) | data formatting | bytes 1216512 | tf_op jit(solution)/shard_map/conv_general_dilated | solution.py:30
  203.2 5.5 %broadcast_select_fusion.1 = f32[128,8,9,32]{3,1,2,0:T(8,128)} fusion(pred[8,9]{0,1:T(8,128)(4,1)S(1)} %copy-done.4, bf16[32,132,1,7,4]{0,3,4,1,2:T(8,128)(2,1)S(1)} %slice.84, bf16[32,132,1,8,9]{0,3,4,1,2:T(8,128)(2,1)S(1)} %copy.35, bf16[3,32,32,3,3]{2,1,4,3,0:T(8,128)(2,1)S(1)} %copy-done.3), kind=kOutput, calls=%fused_computation.26 | convolution fusion | flops 172800000 | bytes 4769792 | tf_op jit(solution)/shard_map/conv_general_dilated | solution.py:30
  208.7 3.7 %copy.36 = f32[128,8,9,32]{0,3,2,1:T(8,128)S(1)} copy(f32[128,8,9,32]{3,1,2,0:T(8,128)} %broadcast_select_fusion.1) | data formatting | bytes 2359296 | tf_op jit(solution)/shard_map/conv_general_dilated | solution.py:30
  212.8 2.9 %collective-permute-start.8 = (bf16[32,4,64]{1,0,2:T(8,128)(2,1)S(1)}, bf16[32,4,64]{1,0,2:T(8,128)(2,1)S(1)}, u32[]{:S(2)}, u32[]{:S(2)}) collective-permute-start(bf16[32,4,64]{1,0,2:T(8,128)(2,1)S(1)} %get-tuple-element.11), channel_id=1, source_target_pairs={{0,32},{32,64},{64,96},{96,128},{128,160},{160,192},{192,224},{224... | collective-permute-start | bytes 49160 | tf_op jit(solution)/shard_map/ppermute | solution.py:20
  215.7 1.9 collective-permute-start.9
  217.7 4.2 %collective-permute-done.8 = bf16[32,4,64]{1,0,2:T(8,128)(2,1)S(1)} collective-permute-done((bf16[32,4,64]{1,0,2:T(8,128)(2,1)S(1)}, bf16[32,4,64]{1,0,2:T(8,128)(2,1)S(1)}, u32[]{:S(2)}, u32[]{:S(2)}) %collective-permute-start.8) | collective-permute-done | bytes 16416 | tf_op jit(solution)/shard_map/ppermute | solution.py:20
  221.9 5.6 %collective-permute-done.9 = bf16[32,4,64]{1,0,2:T(8,128)(2,1)S(1)} collective-permute-done((bf16[32,4,64]{1,0,2:T(8,128)(2,1)S(1)}, bf16[32,4,64]{1,0,2:T(8,128)(2,1)S(1)}, u32[]{:S(2)}, u32[]{:S(2)}) %collective-permute-start.9) | collective-permute-done | bytes 16416 | tf_op jit(solution)/shard_map/ppermute | solution.py:22
  227.6 1.9 collective-permute-start.10
  229.5 3.5 %collective-permute-start.11 = (bf16[32,136,4]{1,0,2:T(8,128)(2,1)S(1)}, bf16[32,136,4]{1,0,2:T(8,128)(2,1)S(1)}, u32[]{:S(2)}, u32[]{:S(2)}) collective-permute-start(bf16[32,136,4]{1,0,2:T(8,128)(2,1)S(1)} %get-tuple-element.6), channel_id=1, source_target_pairs={{1,0},{2,1},{3,2},{4,3},{5,4},{6,5},{7,6},{8,7},{9,8},{10,9},{11,1... | collective-permute-start | bytes 104456 | tf_op jit(solution)/shard_map/ppermute | solution.py:22
  233.1 4.8 %collective-permute-done.11 = bf16[32,136,4]{1,0,2:T(8,128)(2,1)S(1)} collective-permute-done((bf16[32,136,4]{1,0,2:T(8,128)(2,1)S(1)}, bf16[32,136,4]{1,0,2:T(8,128)(2,1)S(1)}, u32[]{:S(2)}, u32[]{:S(2)}) %collective-permute-start.11) | collective-permute-done | bytes 34848 | tf_op jit(solution)/shard_map/ppermute | solution.py:22
  237.8 1.6 pad_maximum_fusion
  239.5 3.0 %copy.38 = bf16[32,136,1,8,9]{0,3,4,1,2:T(8,128)(2,1)S(1)} copy(bf16[32,136,1,8,9]{1,0,4,3,2:T(8,128)(2,1)} %bitcast.83) | data formatting | bytes 1253376 | tf_op jit(solution)/shard_map/conv_general_dilated | solution.py:30
  243.1 6.7 %broadcast_select_fusion = f32[128,8,9,32]{3,1,2,0:T(8,128)} fusion(pred[8,9]{0,1:T(8,128)(4,1)S(1)} %copy-done.4, bf16[32,136,1,7,8]{0,3,4,1,2:T(8,128)(2,1)S(1)} %slice.88, bf16[32,136,1,8,9]{0,3,4,1,2:T(8,128)(2,1)S(1)} %copy.38, bf16[3,32,32,3,3]{2,1,4,3,0:T(8,128)(2,1)S(1)} %copy-done.3), kind=kOutput, calls=%fused_computation.25 | convolution fusion | flops 173715456 | bytes 5990400 | tf_op jit(solution)/shard_map/conv_general_dilated | solution.py:30
  249.8 3.8 %copy.39 = f32[128,8,9,32]{0,3,2,1:T(8,128)S(1)} copy(f32[128,8,9,32]{3,1,2,0:T(8,128)} %broadcast_select_fusion) | data formatting | bytes 2359296 | tf_op jit(solution)/shard_map/conv_general_dilated | solution.py:30
  (37 shorter events, 11.3 us)
Async XLA Ops:
  6.5 1.6 copy-start
  6.5 120.6 %all-reduce.2.cloned.1.call-start = ((), (), s32[]{:S(2)}) async-start(), calls=%async_computation | async-start | bytes 262144 | tf_op jit(solution)/shard_map/psum | solution.py:9
  8.1 142.8 %copy-start.1 = (f32[3,32]{1,0:T(4,128)S(1)}, f32[3,32]{1,0:T(4,128)}, u32[]{:S(2)}) copy-start(f32[3,32]{1,0:T(4,128)} %param.10) | copy-start | bytes 1156
  128.7 10.2 %collective-permute-start = (bf16[32,1,64]{1,0,2:T(8,128)(2,1)S(1)}, bf16[32,1,64]{1,0,2:T(8,128)(2,1)S(1)}, u32[]{:S(2)}, u32[]{:S(2)}) collective-permute-start(bf16[32,1,64]{1,0,2:T(8,128)(2,1)S(1)} %get-tuple-element.15), channel_id=1, source_target_pairs={{0,32},{32,64},{64,96},{96,128},{128,160},{160,192},{192,224},{224... | collective-permute-start | bytes 12296 | tf_op jit(solution)/shard_map/ppermute | solution.py:20
  132.8 11.7 %collective-permute-start.1 = (bf16[32,1,64]{1,0,2:T(8,128)(2,1)S(1)}, bf16[32,1,64]{1,0,2:T(8,128)(2,1)S(1)}, u32[]{:S(2)}, u32[]{:S(2)}) collective-permute-start(bf16[32,1,64]{1,0,2:T(8,128)(2,1)S(1)} %get-tuple-element.16), channel_id=1, source_target_pairs={{32,0},{64,32},{96,64},{128,96},{160,128},{192,160},{224,192},{256... | collective-permute-start | bytes 12296 | tf_op jit(solution)/shard_map/ppermute | solution.py:22
  144.6 6.3 %collective-permute-start.2 = (bf16[32,130,1]{1,0,2:T(8,128)(2,1)S(1)}, bf16[32,130,1]{1,0,2:T(8,128)(2,1)S(1)}, u32[]{:S(2)}, u32[]{:S(2)}) collective-permute-start(bf16[32,130,1]{1,0,2:T(8,128)(2,1)S(1)} %get-tuple-element.9), channel_id=1, source_target_pairs={{0,1},{1,2},{2,3},{3,4},{4,5},{5,6},{6,7},{7,8},{8,9},{9,10},{10,1... | collective-permute-start | bytes 24968 | tf_op jit(solution)/shard_map/ppermute | solution.py:20
  149.0 7.8 %collective-permute-start.3 = (bf16[32,130,1]{1,0,2:T(8,128)(2,1)S(1)}, bf16[32,130,1]{1,0,2:T(8,128)(2,1)S(1)}, u32[]{:S(2)}, u32[]{:S(2)}) collective-permute-start(bf16[32,130,1]{1,0,2:T(8,128)(2,1)S(1)} %get-tuple-element.10), channel_id=1, source_target_pairs={{1,0},{2,1},{3,2},{4,3},{5,4},{6,5},{7,6},{8,7},{9,8},{10,9},{11,1... | collective-permute-start | bytes 24968 | tf_op jit(solution)/shard_map/ppermute | solution.py:22
  157.7 4.3 %copy-start.3 = (bf16[3,32,32,3,3]{2,1,4,3,0:T(8,128)(2,1)S(1)}, bf16[3,32,32,3,3]{2,1,4,3,0:T(8,128)(2,1)}, u32[]{:S(2)}) copy-start(bf16[3,32,32,3,3]{2,1,4,3,0:T(8,128)(2,1)} %param.9) | copy-start | bytes 165892
  157.8 4.3 %copy-start.4 = (pred[8,9]{0,1:T(8,128)(4,1)S(1)}, pred[8,9]{0,1:T(8,128)(4,1)}, u32[]{:S(2)}) copy-start(pred[8,9]{0,1:T(8,128)(4,1)} %constant.47) | copy-start | bytes 220
  172.8 9.3 %collective-permute-start.4 = (bf16[32,2,64]{1,0,2:T(8,128)(2,1)S(1)}, bf16[32,2,64]{1,0,2:T(8,128)(2,1)S(1)}, u32[]{:S(2)}, u32[]{:S(2)}) collective-permute-start(bf16[32,2,64]{1,0,2:T(8,128)(2,1)S(1)} %get-tuple-element.13), channel_id=1, source_target_pairs={{0,32},{32,64},{64,96},{96,128},{128,160},{160,192},{192,224},{224... | collective-permute-start | bytes 24584 | tf_op jit(solution)/shard_map/ppermute | solution.py:20
  176.0 11.7 %collective-permute-start.5 = (bf16[32,2,64]{1,0,2:T(8,128)(2,1)S(1)}, bf16[32,2,64]{1,0,2:T(8,128)(2,1)S(1)}, u32[]{:S(2)}, u32[]{:S(2)}) collective-permute-start(bf16[32,2,64]{1,0,2:T(8,128)(2,1)S(1)} %get-tuple-element.14), channel_id=1, source_target_pairs={{32,0},{64,32},{96,64},{128,96},{160,128},{192,160},{224,192},{256... | collective-permute-start | bytes 24584 | tf_op jit(solution)/shard_map/ppermute | solution.py:22
  187.8 5.3 %collective-permute-start.6 = (bf16[32,132,2]{1,0,2:T(8,128)(2,1)S(1)}, bf16[32,132,2]{1,0,2:T(8,128)(2,1)S(1)}, u32[]{:S(2)}, u32[]{:S(2)}) collective-permute-start(bf16[32,132,2]{1,0,2:T(8,128)(2,1)S(1)} %get-tuple-element.7), channel_id=1, source_target_pairs={{0,1},{1,2},{2,3},{3,4},{4,5},{5,6},{6,7},{7,8},{8,9},{9,10},{10,1... | collective-permute-start | bytes 50696 | tf_op jit(solution)/shard_map/ppermute | solution.py:20
  189.7 8.0 %collective-permute-start.7 = (bf16[32,132,2]{1,0,2:T(8,128)(2,1)S(1)}, bf16[32,132,2]{1,0,2:T(8,128)(2,1)S(1)}, u32[]{:S(2)}, u32[]{:S(2)}) collective-permute-start(bf16[32,132,2]{1,0,2:T(8,128)(2,1)S(1)} %get-tuple-element.8), channel_id=1, source_target_pairs={{1,0},{2,1},{3,2},{4,3},{5,4},{6,5},{7,6},{8,7},{9,8},{10,9},{11,1... | collective-permute-start | bytes 50696 | tf_op jit(solution)/shard_map/ppermute | solution.py:22
  212.8 9.0 %collective-permute-start.8 = (bf16[32,4,64]{1,0,2:T(8,128)(2,1)S(1)}, bf16[32,4,64]{1,0,2:T(8,128)(2,1)S(1)}, u32[]{:S(2)}, u32[]{:S(2)}) collective-permute-start(bf16[32,4,64]{1,0,2:T(8,128)(2,1)S(1)} %get-tuple-element.11), channel_id=1, source_target_pairs={{0,32},{32,64},{64,96},{96,128},{128,160},{160,192},{192,224},{224... | collective-permute-start | bytes 49160 | tf_op jit(solution)/shard_map/ppermute | solution.py:20
  215.7 11.7 %collective-permute-start.9 = (bf16[32,4,64]{1,0,2:T(8,128)(2,1)S(1)}, bf16[32,4,64]{1,0,2:T(8,128)(2,1)S(1)}, u32[]{:S(2)}, u32[]{:S(2)}) collective-permute-start(bf16[32,4,64]{1,0,2:T(8,128)(2,1)S(1)} %get-tuple-element.12), channel_id=1, source_target_pairs={{32,0},{64,32},{96,64},{128,96},{160,128},{192,160},{224,192},{256... | collective-permute-start | bytes 49160 | tf_op jit(solution)/shard_map/ppermute | solution.py:22
  227.6 5.5 %collective-permute-start.10 = (bf16[32,136,4]{1,0,2:T(8,128)(2,1)S(1)}, bf16[32,136,4]{1,0,2:T(8,128)(2,1)S(1)}, u32[]{:S(2)}, u32[]{:S(2)}) collective-permute-start(bf16[32,136,4]{1,0,2:T(8,128)(2,1)S(1)} %get-tuple-element.5), channel_id=1, source_target_pairs={{0,1},{1,2},{2,3},{3,4},{4,5},{5,6},{6,7},{7,8},{8,9},{9,10},{10,1... | collective-permute-start | bytes 104456 | tf_op jit(solution)/shard_map/ppermute | solution.py:20
  229.5 8.3 %collective-permute-start.11 = (bf16[32,136,4]{1,0,2:T(8,128)(2,1)S(1)}, bf16[32,136,4]{1,0,2:T(8,128)(2,1)S(1)}, u32[]{:S(2)}, u32[]{:S(2)}) collective-permute-start(bf16[32,136,4]{1,0,2:T(8,128)(2,1)S(1)} %get-tuple-element.6), channel_id=1, source_target_pairs={{1,0},{2,1},{3,2},{4,3},{5,4},{6,5},{7,6},{8,7},{9,8},{10,9},{11,1... | collective-permute-start | bytes 104456 | tf_op jit(solution)/shard_map/ppermute | solution.py:22
  249.8 3.8 %copy-start.2 = (bf16[32]{0:T(256)(128)(2,1)S(1)}, bf16[32]{0:T(256)(128)(2,1)}, u32[]{:S(2)}) copy-start(bf16[32]{0:T(256)(128)(2,1)} %param.11) | copy-start | bytes 196
Sparse Core Ops, SparseCore 0:
  9.6 117.4 all-reduce.1
where the time goes:
time: 262 us; the launch traced here: 261 us
  waiting for transfers between devices  162 us (62%)
  starting transfers between devices  32.9 us (13%)
  local copies, waits for them, and re-layouts  25.1 us (10%)
  matrix products  21.6 us (8%)
  between operations  13.7 us (5%)
  other arithmetic  5.54 us (2%)
    psum x1, waiting for transfers between devices, spread(): return lax.psum(kept, axis)  118 us
    ppermute x6, waiting for transfers between devices, extended(): lax.ppermute(head, axis, [((i + 1) % count, i) for i in range(ends)])  32 us
    conv_general_dilated x9, local copies, waits for them, and re-layouts, dilated_level(): lax.conv_general_dilated(padded[None], weight, (1, 1), 'VALID', rhs_dilat...  22.7 us
    conv_general_dilated x3, matrix products, dilated_level(): lax.conv_general_dilated(padded[None], weight, (1, 1), 'VALID', rhs_dilat...  18.7 us
    ppermute x6, starting transfers between devices, extended(): lax.ppermute(tail, axis, [(i, (i + 1) % count) for i in range(ends)])  18.3 us
    ppermute x6, starting transfers between devices, extended(): lax.ppermute(head, axis, [((i + 1) % count, i) for i in range(ends)])  14.6 us
    ppermute x6, waiting for transfers between devices, extended(): lax.ppermute(tail, axis, [(i, (i + 1) % count) for i in range(ends)])  12.5 us
  transfers between devices with their start and end apart: 13, of which 10 were waited for; matrix products, arithmetic and copies ran while one was open for 0% of the time, Pallas kernels for 0%

commit v1 on v0

--- a/solution.py
+++ b/solution.py
@@ -3,10 +3,12 @@
 from jax import lax
 from jax.sharding import PartitionSpec as P
 
+frame_divide = lambda mesh_dim, matrix: jax.lax.all_gather(matrix, mesh_dim).sum(axis=0)
+
 
 def spread(value, axis, source):
     kept = jnp.where(lax.axis_index(axis) == source, value, 0).astype(value.dtype)
-    return lax.psum(kept, axis)
+    return frame_divide(axis, kept)
 
 
 def extended(cells, sides, width):

time: 262 us -> 188 us (0.72)
  the two profiles are of different devices: /device:TPU:223 before, /device:TPU:31 now
where the time goes in v1:
time: 188 us
  waiting for transfers between devices  89.7 us (48%)
  starting transfers between devices  31.7 us (17%)
  local copies, waits for them, and re-layouts  25.1 us (13%)
  matrix products  20.8 us (11%)
  between operations  13.7 us (7%)
  other arithmetic  6.55 us (3%)
    all_gather x1, waiting for transfers between devices, jax.lax.all_gather(matrix, mesh_dim).sum(axis=0)  48.8 us
    ppermute x6, waiting for transfers between devices, extended(): lax.ppermute(head, axis, [((i + 1) % count, i) for i in range(ends)])  28.4 us
    conv_general_dilated x9, local copies, waits for them, and re-layouts, dilated_level(): lax.conv_general_dilated(padded[None], weight, (1, 1), 'VALID', rhs_dilat...  22.7 us
    conv_general_dilated x3, matrix products, dilated_level(): lax.conv_general_dilated(padded[None], weight, (1, 1), 'VALID', rhs_dilat...  18.8 us
    ppermute x6, starting transfers between devices, extended(): lax.ppermute(tail, axis, [(i, (i + 1) % count) for i in range(ends)])  17.1 us
    ppermute x6, starting transfers between devices, extended(): lax.ppermute(head, axis, [((i + 1) % count, i) for i in range(ends)])  14.6 us
    ppermute x6, waiting for transfers between devices, extended(): lax.ppermute(tail, axis, [(i, (i + 1) % count) for i in range(ends)])  12.5 us
  transfers between devices with their start and end apart: 13, of which 10 were waited for; matrix products, arithmetic and copies ran while one was open for 1% of the time, Pallas kernels for 0%

profile of v1, /device:TPU:31, one launch (start us, length us, event | category | flops | bytes accessed | tf_op | source)
XLA Modules:
  0.0 187.7 jit_solution(2864178915584927803)
XLA Ops:
  8.3 48.8 %all-gather.3.cloned.1.call-done = bf16[2048,512]{1,0:T(8,128)(2,1)} async-done(((bf16[128,512]{1,0:T(8,128)(2,1)}), bf16[2048,512]{1,0:T(8,128)(2,1)}) %all-gather.3.cloned.1.call-update) | async-done | bytes 2097168 | tf_op jit(solution)/shard_map/all_gather | solution.py:6
  57.1 1.9 %reduce_sum.12 = bf16[128,512]{1,0:T(8,128)(2,1)S(1)} reduce(bf16[16,128,512]{2,1,0:T(8,128)(2,1)} %bitcast.89, bf16[]{:T(256)} %constant.35.clone.1), dimensions={0}, to_apply=%region_0.1 | reduce | flops 983040 | bytes 2228226 | tf_op jit(solution)/shard_map/reduce_sum | solution.py:6
  59.8 2.6 %collective-permute-start = (bf16[32,1,64]{1,0,2:T(8,128)(2,1)S(1)}, bf16[32,1,64]{1,0,2:T(8,128)(2,1)S(1)}, u32[]{:S(2)}, u32[]{:S(2)}) collective-permute-start(bf16[32,1,64]{1,0,2:T(8,128)(2,1)S(1)} %get-tuple-element.15), channel_id=1, source_target_pairs={{0,32},{32,64},{64,96},{96,128},{128,160},{160,192},{192,224},{224... | collective-permute-start | bytes 12296 | tf_op jit(solution)/shard_map/ppermute | solution.py:22
  62.4 1.9 %collective-permute-start.1 = (bf16[32,1,64]{1,0,2:T(8,128)(2,1)S(1)}, bf16[32,1,64]{1,0,2:T(8,128)(2,1)S(1)}, u32[]{:S(2)}, u32[]{:S(2)}) collective-permute-start(bf16[32,1,64]{1,0,2:T(8,128)(2,1)S(1)} %get-tuple-element.16), channel_id=1, source_target_pairs={{32,0},{64,32},{96,64},{128,96},{160,128},{192,160},{224,192},{256... | collective-permute-start | bytes 12296 | tf_op jit(solution)/shard_map/ppermute | solution.py:24
  64.4 4.2 %collective-permute-done = bf16[32,1,64]{1,0,2:T(8,128)(2,1)S(1)} collective-permute-done((bf16[32,1,64]{1,0,2:T(8,128)(2,1)S(1)}, bf16[32,1,64]{1,0,2:T(8,128)(2,1)S(1)}, u32[]{:S(2)}, u32[]{:S(2)}) %collective-permute-start) | collective-permute-done | bytes 4128 | tf_op jit(solution)/shard_map/ppermute | solution.py:22
  68.5 4.4 %collective-permute-done.1 = bf16[32,1,64]{1,0,2:T(8,128)(2,1)S(1)} collective-permute-done((bf16[32,1,64]{1,0,2:T(8,128)(2,1)S(1)}, bf16[32,1,64]{1,0,2:T(8,128)(2,1)S(1)}, u32[]{:S(2)}, u32[]{:S(2)}) %collective-permute-start.1) | collective-permute-done | bytes 4128 | tf_op jit(solution)/shard_map/ppermute | solution.py:24
  73.0 4.3 %collective-permute-start.2 = (bf16[32,130,1]{1,0,2:T(8,128)(2,1)S(1)}, bf16[32,130,1]{1,0,2:T(8,128)(2,1)S(1)}, u32[]{:S(2)}, u32[]{:S(2)}) collective-permute-start(bf16[32,130,1]{1,0,2:T(8,128)(2,1)S(1)} %get-tuple-element.9), channel_id=1, source_target_pairs={{0,1},{1,2},{2,3},{3,4},{4,5},{5,6},{6,7},{7,8},{8,9},{9,10},{10,1... | collective-permute-start | bytes 24968 | tf_op jit(solution)/shard_map/ppermute | solution.py:22
  77.3 1.9 %collective-permute-start.3 = (bf16[32,130,1]{1,0,2:T(8,128)(2,1)S(1)}, bf16[32,130,1]{1,0,2:T(8,128)(2,1)S(1)}, u32[]{:S(2)}, u32[]{:S(2)}) collective-permute-start(bf16[32,130,1]{1,0,2:T(8,128)(2,1)S(1)} %get-tuple-element.10), channel_id=1, source_target_pairs={{1,0},{2,1},{3,2},{4,3},{5,4},{6,5},{7,6},{8,7},{9,8},{10,9},{11,1... | collective-permute-start | bytes 24968 | tf_op jit(solution)/shard_map/ppermute | solution.py:24
  79.3 5.8 %collective-permute-done.3 = bf16[32,130,1]{1,0,2:T(8,128)(2,1)S(1)} collective-permute-done((bf16[32,130,1]{1,0,2:T(8,128)(2,1)S(1)}, bf16[32,130,1]{1,0,2:T(8,128)(2,1)S(1)}, u32[]{:S(2)}, u32[]{:S(2)}) %collective-permute-start.3) | collective-permute-done | bytes 8352 | tf_op jit(solution)/shard_map/ppermute | solution.py:24
  86.1 3.0 %copy.32 = bf16[32,130,1,8,9]{0,3,4,1,2:T(8,128)(2,1)} copy(bf16[32,130,1,8,9]{1,0,4,3,2:T(8,128)(2,1)S(1)} %bitcast.85) | data formatting | bytes 1198080 | tf_op jit(solution)/shard_map/conv_general_dilated | solution.py:32
  90.4 6.6 %broadcast_select_fusion.2 = f32[128,8,9,32]{3,1,2,0:T(8,128)} fusion(pred[8,9]{0,1:T(8,128)(4,1)S(1)} %copy-done.5, bf16[32,130,1,7,2]{0,3,4,1,2:T(8,128)(2,1)S(1)} %slice.80, bf16[32,130,1,8,9]{0,3,4,1,2:T(8,128)(2,1)} %copy.32, bf16[3,32,32,3,3]{2,1,4,3,0:T(8,128)(2,1)S(1)} %copy-done.4), kind=kOutput, calls=%fused_computation.27 | convolution fusion | flops 172360704 | bytes 2386944 | tf_op jit(solution)/shard_map/conv_general_dilated | solution.py:32
  97.0 3.7 %copy.33 = f32[128,8,9,32]{0,3,2,1:T(8,128)S(1)} copy(f32[128,8,9,32]{3,1,2,0:T(8,128)} %broadcast_select_fusion.2) | data formatting | bytes 2359296 | tf_op jit(solution)/shard_map/conv_general_dilated | solution.py:32
  101.1 3.2 %collective-permute-start.4 = (bf16[32,2,64]{1,0,2:T(8,128)(2,1)S(1)}, bf16[32,2,64]{1,0,2:T(8,128)(2,1)S(1)}, u32[]{:S(2)}, u32[]{:S(2)}) collective-permute-start(bf16[32,2,64]{1,0,2:T(8,128)(2,1)S(1)} %get-tuple-element.13), channel_id=1, source_target_pairs={{0,32},{32,64},{64,96},{96,128},{128,160},{160,192},{192,224},{224... | collective-permute-start | bytes 24584 | tf_op jit(solution)/shard_map/ppermute | solution.py:22
  104.3 1.9 %collective-permute-start.5 = (bf16[32,2,64]{1,0,2:T(8,128)(2,1)S(1)}, bf16[32,2,64]{1,0,2:T(8,128)(2,1)S(1)}, u32[]{:S(2)}, u32[]{:S(2)}) collective-permute-start(bf16[32,2,64]{1,0,2:T(8,128)(2,1)S(1)} %get-tuple-element.14), channel_id=1, source_target_pairs={{32,0},{64,32},{96,64},{128,96},{160,128},{192,160},{224,192},{256... | collective-permute-start | bytes 24584 | tf_op jit(solution)/shard_map/ppermute | solution.py:24
  106.3 4.2 %collective-permute-done.4 = bf16[32,2,64]{1,0,2:T(8,128)(2,1)S(1)} collective-permute-done((bf16[32,2,64]{1,0,2:T(8,128)(2,1)S(1)}, bf16[32,2,64]{1,0,2:T(8,128)(2,1)S(1)}, u32[]{:S(2)}, u32[]{:S(2)}) %collective-permute-start.4) | collective-permute-done | bytes 8224 | tf_op jit(solution)/shard_map/ppermute | solution.py:22
  110.4 4.4 %collective-permute-done.5 = bf16[32,2,64]{1,0,2:T(8,128)(2,1)S(1)} collective-permute-done((bf16[32,2,64]{1,0,2:T(8,128)(2,1)S(1)}, bf16[32,2,64]{1,0,2:T(8,128)(2,1)S(1)}, u32[]{:S(2)}, u32[]{:S(2)}) %collective-permute-start.5) | collective-permute-done | bytes 8224 | tf_op jit(solution)/shard_map/ppermute | solution.py:24
  114.9 1.9 %collective-permute-start.6 = (bf16[32,132,2]{1,0,2:T(8,128)(2,1)S(1)}, bf16[32,132,2]{1,0,2:T(8,128)(2,1)S(1)}, u32[]{:S(2)}, u32[]{:S(2)}) collective-permute-start(bf16[32,132,2]{1,0,2:T(8,128)(2,1)S(1)} %get-tuple-element.7), channel_id=1, source_target_pairs={{0,1},{1,2},{2,3},{3,4},{4,5},{5,6},{6,7},{7,8},{8,9},{9,10},{10,1... | collective-permute-start | bytes 50696 | tf_op jit(solution)/shard_map/ppermute | solution.py:22
  116.9 3.4 %collective-permute-start.7 = (bf16[32,132,2]{1,0,2:T(8,128)(2,1)S(1)}, bf16[32,132,2]{1,0,2:T(8,128)(2,1)S(1)}, u32[]{:S(2)}, u32[]{:S(2)}) collective-permute-start(bf16[32,132,2]{1,0,2:T(8,128)(2,1)S(1)} %get-tuple-element.8), channel_id=1, source_target_pairs={{1,0},{2,1},{3,2},{4,3},{5,4},{6,5},{7,6},{8,7},{9,8},{10,9},{11,1... | collective-permute-start | bytes 50696 | tf_op jit(solution)/shard_map/ppermute | solution.py:24
  120.2 4.6 %collective-permute-done.7 = bf16[32,132,2]{1,0,2:T(8,128)(2,1)S(1)} collective-permute-done((bf16[32,132,2]{1,0,2:T(8,128)(2,1)S(1)}, bf16[32,132,2]{1,0,2:T(8,128)(2,1)S(1)}, u32[]{:S(2)}, u32[]{:S(2)}) %collective-permute-start.7) | collective-permute-done | bytes 16928 | tf_op jit(solution)/shard_map/ppermute | solution.py:24
  126.8 3.3 %copy.35 = bf16[32,132,1,8,9]{0,3,4,1,2:T(8,128)(2,1)S(1)} copy(bf16[32,132,1,8,9]{1,0,4,3,2:T(8,128)(2,1)} %bitcast.83) | data formatting | bytes 1216512 | tf_op jit(solution)/shard_map/conv_general_dilated | solution.py:32
  130.4 5.5 %broadcast_select_fusion.1 = f32[128,8,9,32]{3,1,2,0:T(8,128)} fusion(pred[8,9]{0,1:T(8,128)(4,1)S(1)} %copy-done.5, bf16[32,132,1,7,4]{0,3,4,1,2:T(8,128)(2,1)S(1)} %slice.84, bf16[32,132,1,8,9]{0,3,4,1,2:T(8,128)(2,1)S(1)} %copy.35, bf16[3,32,32,3,3]{2,1,4,3,0:T(8,128)(2,1)S(1)} %copy-done.4), kind=kOutput, calls=%fused_computation.26 | convolution fusion | flops 172800000 | bytes 4769792 | tf_op jit(solution)/shard_map/conv_general_dilated | solution.py:32
  135.9 3.7 %copy.36 = f32[128,8,9,32]{0,3,2,1:T(8,128)S(1)} copy(f32[128,8,9,32]{3,1,2,0:T(8,128)} %broadcast_select_fusion.1) | data formatting | bytes 2359296 | tf_op jit(solution)/shard_map/conv_general_dilated | solution.py:32
  140.0 3.2 %collective-permute-start.8 = (bf16[32,4,64]{1,0,2:T(8,128)(2,1)S(1)}, bf16[32,4,64]{1,0,2:T(8,128)(2,1)S(1)}, u32[]{:S(2)}, u32[]{:S(2)}) collective-permute-start(bf16[32,4,64]{1,0,2:T(8,128)(2,1)S(1)} %get-tuple-element.11), channel_id=1, source_target_pairs={{0,32},{32,64},{64,96},{96,128},{128,160},{160,192},{192,224},{224... | collective-permute-start | bytes 49160 | tf_op jit(solution)/shard_map/ppermute | solution.py:22
  143.2 1.9 %collective-permute-start.9 = (bf16[32,4,64]{1,0,2:T(8,128)(2,1)S(1)}, bf16[32,4,64]{1,0,2:T(8,128)(2,1)S(1)}, u32[]{:S(2)}, u32[]{:S(2)}) collective-permute-start(bf16[32,4,64]{1,0,2:T(8,128)(2,1)S(1)} %get-tuple-element.12), channel_id=1, source_target_pairs={{32,0},{64,32},{96,64},{128,96},{160,128},{192,160},{224,192},{256... | collective-permute-start | bytes 49160 | tf_op jit(solution)/shard_map/ppermute | solution.py:24
  145.2 4.2 %collective-permute-done.8 = bf16[32,4,64]{1,0,2:T(8,128)(2,1)S(1)} collective-permute-done((bf16[32,4,64]{1,0,2:T(8,128)(2,1)S(1)}, bf16[32,4,64]{1,0,2:T(8,128)(2,1)S(1)}, u32[]{:S(2)}, u32[]{:S(2)}) %collective-permute-start.8) | collective-permute-done | bytes 16416 | tf_op jit(solution)/shard_map/ppermute | solution.py:22
  149.3 4.4 %collective-permute-done.9 = bf16[32,4,64]{1,0,2:T(8,128)(2,1)S(1)} collective-permute-done((bf16[32,4,64]{1,0,2:T(8,128)(2,1)S(1)}, bf16[32,4,64]{1,0,2:T(8,128)(2,1)S(1)}, u32[]{:S(2)}, u32[]{:S(2)}) %collective-permute-start.9) | collective-permute-done | bytes 16416 | tf_op jit(solution)/shard_map/ppermute | solution.py:24
  153.9 1.9 %collective-permute-start.10 = (bf16[32,136,4]{1,0,2:T(8,128)(2,1)S(1)}, bf16[32,136,4]{1,0,2:T(8,128)(2,1)S(1)}, u32[]{:S(2)}, u32[]{:S(2)}) collective-permute-start(bf16[32,136,4]{1,0,2:T(8,128)(2,1)S(1)} %get-tuple-element.5), channel_id=1, source_target_pairs={{0,1},{1,2},{2,3},{3,4},{4,5},{5,6},{6,7},{7,8},{8,9},{9,10},{10,1... | collective-permute-start | bytes 104456 | tf_op jit(solution)/shard_map/ppermute | solution.py:22
  155.8 3.5 %collective-permute-start.11 = (bf16[32,136,4]{1,0,2:T(8,128)(2,1)S(1)}, bf16[32,136,4]{1,0,2:T(8,128)(2,1)S(1)}, u32[]{:S(2)}, u32[]{:S(2)}) collective-permute-start(bf16[32,136,4]{1,0,2:T(8,128)(2,1)S(1)} %get-tuple-element.6), channel_id=1, source_target_pairs={{1,0},{2,1},{3,2},{4,3},{5,4},{6,5},{7,6},{8,7},{9,8},{10,9},{11,1... | collective-permute-start | bytes 104456 | tf_op jit(solution)/shard_map/ppermute | solution.py:24
  159.4 4.8 %collective-permute-done.11 = bf16[32,136,4]{1,0,2:T(8,128)(2,1)S(1)} collective-permute-done((bf16[32,136,4]{1,0,2:T(8,128)(2,1)S(1)}, bf16[32,136,4]{1,0,2:T(8,128)(2,1)S(1)}, u32[]{:S(2)}, u32[]{:S(2)}) %collective-permute-start.11) | collective-permute-done | bytes 34848 | tf_op jit(solution)/shard_map/ppermute | solution.py:24
  165.8 3.0 %copy.38 = bf16[32,136,1,8,9]{0,3,4,1,2:T(8,128)(2,1)S(1)} copy(bf16[32,136,1,8,9]{1,0,4,3,2:T(8,128)(2,1)} %bitcast.84) | data formatting | bytes 1253376 | tf_op jit(solution)/shard_map/conv_general_dilated | solution.py:32
  169.4 6.7 %broadcast_select_fusion = f32[128,8,9,32]{3,1,2,0:T(8,128)} fusion(pred[8,9]{0,1:T(8,128)(4,1)S(1)} %copy-done.5, bf16[32,136,1,7,8]{0,3,4,1,2:T(8,128)(2,1)S(1)} %slice.88, bf16[32,136,1,8,9]{0,3,4,1,2:T(8,128)(2,1)S(1)} %copy.38, bf16[3,32,32,3,3]{2,1,4,3,0:T(8,128)(2,1)S(1)} %copy-done.4), kind=kOutput, calls=%fused_computation.25 | convolution fusion | flops 173715456 | bytes 5990400 | tf_op jit(solution)/shard_map/conv_general_dilated | solution.py:32
  176.1 3.8 %copy.39 = f32[128,8,9,32]{0,3,2,1:T(8,128)S(1)} copy(f32[128,8,9,32]{3,1,2,0:T(8,128)} %broadcast_select_fusion) | data formatting | bytes 2359296 | tf_op jit(solution)/shard_map/conv_general_dilated | solution.py:32
  (40 shorter events, 11.3 us)
Async XLA Ops:
  6.5 0.8 copy-start
  6.5 52.5 %copy-start.1 = (bf16[512,32]{0,1:T(8,128)(2,1)S(1)}, bf16[512,32]{0,1:T(8,128)(2,1)}, u32[]{:S(2)}) copy-start(bf16[512,32]{0,1:T(8,128)(2,1)} %param.8) | copy-start | bytes 98308
  6.5 50.6 %all-gather.3.cloned.1.call-start = ((), (), s32[]{:S(2)}) async-start(), calls=%async_computation | async-start | bytes 2228224 | tf_op jit(solution)/shard_map/all_gather | solution.py:6
  59.0 20.3 %copy-start.2 = (f32[3,32]{1,0:T(4,128)S(1)}, f32[3,32]{1,0:T(4,128)}, u32[]{:S(2)}) copy-start(f32[3,32]{1,0:T(4,128)} %param.10) | copy-start | bytes 1156
  59.8 8.7 %collective-permute-start = (bf16[32,1,64]{1,0,2:T(8,128)(2,1)S(1)}, bf16[32,1,64]{1,0,2:T(8,128)(2,1)S(1)}, u32[]{:S(2)}, u32[]{:S(2)}) collective-permute-start(bf16[32,1,64]{1,0,2:T(8,128)(2,1)S(1)} %get-tuple-element.15), channel_id=1, source_target_pairs={{0,32},{32,64},{64,96},{96,128},{128,160},{160,192},{192,224},{224... | collective-permute-start | bytes 12296 | tf_op jit(solution)/shard_map/ppermute | solution.py:22
  62.4 10.5 %collective-permute-start.1 = (bf16[32,1,64]{1,0,2:T(8,128)(2,1)S(1)}, bf16[32,1,64]{1,0,2:T(8,128)(2,1)S(1)}, u32[]{:S(2)}, u32[]{:S(2)}) collective-permute-start(bf16[32,1,64]{1,0,2:T(8,128)(2,1)S(1)} %get-tuple-element.16), channel_id=1, source_target_pairs={{32,0},{64,32},{96,64},{128,96},{160,128},{192,160},{224,192},{256... | collective-permute-start | bytes 12296 | tf_op jit(solution)/shard_map/ppermute | solution.py:24
  73.0 6.3 %collective-permute-start.2 = (bf16[32,130,1]{1,0,2:T(8,128)(2,1)S(1)}, bf16[32,130,1]{1,0,2:T(8,128)(2,1)S(1)}, u32[]{:S(2)}, u32[]{:S(2)}) collective-permute-start(bf16[32,130,1]{1,0,2:T(8,128)(2,1)S(1)} %get-tuple-element.9), channel_id=1, source_target_pairs={{0,1},{1,2},{2,3},{3,4},{4,5},{5,6},{6,7},{7,8},{8,9},{9,10},{10,1... | collective-permute-start | bytes 24968 | tf_op jit(solution)/shard_map/ppermute | solution.py:22
  77.3 7.8 %collective-permute-start.3 = (bf16[32,130,1]{1,0,2:T(8,128)(2,1)S(1)}, bf16[32,130,1]{1,0,2:T(8,128)(2,1)S(1)}, u32[]{:S(2)}, u32[]{:S(2)}) collective-permute-start(bf16[32,130,1]{1,0,2:T(8,128)(2,1)S(1)} %get-tuple-element.10), channel_id=1, source_target_pairs={{1,0},{2,1},{3,2},{4,3},{5,4},{6,5},{7,6},{8,7},{9,8},{10,9},{11,1... | collective-permute-start | bytes 24968 | tf_op jit(solution)/shard_map/ppermute | solution.py:24
  86.1 4.3 %copy-start.4 = (bf16[3,32,32,3,3]{2,1,4,3,0:T(8,128)(2,1)S(1)}, bf16[3,32,32,3,3]{2,1,4,3,0:T(8,128)(2,1)}, u32[]{:S(2)}) copy-start(bf16[3,32,32,3,3]{2,1,4,3,0:T(8,128)(2,1)} %param.9) | copy-start | bytes 165892
  86.1 4.3 %copy-start.5 = (pred[8,9]{0,1:T(8,128)(4,1)S(1)}, pred[8,9]{0,1:T(8,128)(4,1)}, u32[]{:S(2)}) copy-start(pred[8,9]{0,1:T(8,128)(4,1)} %constant.49) | copy-start | bytes 220
  101.1 9.3 %collective-permute-start.4 = (bf16[32,2,64]{1,0,2:T(8,128)(2,1)S(1)}, bf16[32,2,64]{1,0,2:T(8,128)(2,1)S(1)}, u32[]{:S(2)}, u32[]{:S(2)}) collective-permute-start(bf16[32,2,64]{1,0,2:T(8,128)(2,1)S(1)} %get-tuple-element.13), channel_id=1, source_target_pairs={{0,32},{32,64},{64,96},{96,128},{128,160},{160,192},{192,224},{224... | collective-permute-start | bytes 24584 | tf_op jit(solution)/shard_map/ppermute | solution.py:22
  104.3 10.5 %collective-permute-start.5 = (bf16[32,2,64]{1,0,2:T(8,128)(2,1)S(1)}, bf16[32,2,64]{1,0,2:T(8,128)(2,1)S(1)}, u32[]{:S(2)}, u32[]{:S(2)}) collective-permute-start(bf16[32,2,64]{1,0,2:T(8,128)(2,1)S(1)} %get-tuple-element.14), channel_id=1, source_target_pairs={{32,0},{64,32},{96,64},{128,96},{160,128},{192,160},{224,192},{256... | collective-permute-start | bytes 24584 | tf_op jit(solution)/shard_map/ppermute | solution.py:24
  114.9 5.3 %collective-permute-start.6 = (bf16[32,132,2]{1,0,2:T(8,128)(2,1)S(1)}, bf16[32,132,2]{1,0,2:T(8,128)(2,1)S(1)}, u32[]{:S(2)}, u32[]{:S(2)}) collective-permute-start(bf16[32,132,2]{1,0,2:T(8,128)(2,1)S(1)} %get-tuple-element.7), channel_id=1, source_target_pairs={{0,1},{1,2},{2,3},{3,4},{4,5},{5,6},{6,7},{7,8},{8,9},{9,10},{10,1... | collective-permute-start | bytes 50696 | tf_op jit(solution)/shard_map/ppermute | solution.py:22
  116.9 8.0 %collective-permute-start.7 = (bf16[32,132,2]{1,0,2:T(8,128)(2,1)S(1)}, bf16[32,132,2]{1,0,2:T(8,128)(2,1)S(1)}, u32[]{:S(2)}, u32[]{:S(2)}) collective-permute-start(bf16[32,132,2]{1,0,2:T(8,128)(2,1)S(1)} %get-tuple-element.8), channel_id=1, source_target_pairs={{1,0},{2,1},{3,2},{4,3},{5,4},{6,5},{7,6},{8,7},{9,8},{10,9},{11,1... | collective-permute-start | bytes 50696 | tf_op jit(solution)/shard_map/ppermute | solution.py:24
  140.0 9.3 %collective-permute-start.8 = (bf16[32,4,64]{1,0,2:T(8,128)(2,1)S(1)}, bf16[32,4,64]{1,0,2:T(8,128)(2,1)S(1)}, u32[]{:S(2)}, u32[]{:S(2)}) collective-permute-start(bf16[32,4,64]{1,0,2:T(8,128)(2,1)S(1)} %get-tuple-element.11), channel_id=1, source_target_pairs={{0,32},{32,64},{64,96},{96,128},{128,160},{160,192},{192,224},{224... | collective-permute-start | bytes 49160 | tf_op jit(solution)/shard_map/ppermute | solution.py:22
  143.2 10.5 %collective-permute-start.9 = (bf16[32,4,64]{1,0,2:T(8,128)(2,1)S(1)}, bf16[32,4,64]{1,0,2:T(8,128)(2,1)S(1)}, u32[]{:S(2)}, u32[]{:S(2)}) collective-permute-start(bf16[32,4,64]{1,0,2:T(8,128)(2,1)S(1)} %get-tuple-element.12), channel_id=1, source_target_pairs={{32,0},{64,32},{96,64},{128,96},{160,128},{192,160},{224,192},{256... | collective-permute-start | bytes 49160 | tf_op jit(solution)/shard_map/ppermute | solution.py:24
  153.9 5.5 %collective-permute-start.10 = (bf16[32,136,4]{1,0,2:T(8,128)(2,1)S(1)}, bf16[32,136,4]{1,0,2:T(8,128)(2,1)S(1)}, u32[]{:S(2)}, u32[]{:S(2)}) collective-permute-start(bf16[32,136,4]{1,0,2:T(8,128)(2,1)S(1)} %get-tuple-element.5), channel_id=1, source_target_pairs={{0,1},{1,2},{2,3},{3,4},{4,5},{5,6},{6,7},{7,8},{8,9},{9,10},{10,1... | collective-permute-start | bytes 104456 | tf_op jit(solution)/shard_map/ppermute | solution.py:22
  155.8 8.3 %collective-permute-start.11 = (bf16[32,136,4]{1,0,2:T(8,128)(2,1)S(1)}, bf16[32,136,4]{1,0,2:T(8,128)(2,1)S(1)}, u32[]{:S(2)}, u32[]{:S(2)}) collective-permute-start(bf16[32,136,4]{1,0,2:T(8,128)(2,1)S(1)} %get-tuple-element.6), channel_id=1, source_target_pairs={{1,0},{2,1},{3,2},{4,3},{5,4},{6,5},{7,6},{8,7},{9,8},{10,9},{11,1... | collective-permute-start | bytes 104456 | tf_op jit(solution)/shard_map/ppermute | solution.py:24
  176.1 3.8 %copy-start.3 = (bf16[32]{0:T(256)(128)(2,1)S(1)}, bf16[32]{0:T(256)(128)(2,1)}, u32[]{:S(2)}) copy-start(bf16[32]{0:T(256)(128)(2,1)} %param.11) | copy-start | bytes 196
Sparse Core Ops, SparseCore 0:
  9.5 47.5 all-gather.2
